TPU v7x, 32 devices: a whole 2x2x4 slice. The times are simulated.
32 devices in a mesh: dp: 4 (over z), shard: 8 (over y, x, core).
Axes of the slice: x: 2, y: 2, z: 4, core: 2. Of those that a mesh axis runs over, the one named last changes fastest.
Arguments:
- tokens: bfloat16 [16384, 1024], P(('dp', 'shard')), may hold values from -6 to 6
- targets: bfloat16 [16384, 1024], P(('dp', 'shard')), may hold values from -6 to 6
- segments: int32 [16384], P('dp'), may hold values from 0 to 511, as said below
- valid: int32 [16384], P(('dp', 'shard')), may hold values from 0 to 1, as said below
- master: float32 [1024, 12288], P('shard')
- vectors: float32 [13312], P('shard')
- left_stat: float32 [8, 96, 128, 128], P('shard'), as said below
- right_stat: float32 [8, 96, 128, 128], P('shard'), as said below
- left_root: bfloat16 [8, 96, 128, 128], P('shard'), as said below
- right_root: bfloat16 [8, 96, 128, 128], P('shard'), as said below
- vector_stat: float32 [13312], P('shard'), may hold values from 0.01 to 1
Outputs:
- input_grad: float32 [16384, 1024], P(('dp', 'shard'))
- grad_norm: float32 [], replicated
- new_left: float32 [8, 96, 128, 128], P('shard')
- new_right: float32 [8, 96, 128, 128], P('shard')
- new_master: float32 [1024, 12288], P('shard')
- master_copy: bfloat16 [1024, 12288], P('shard')
- new_vectors: float32 [13312], P('shard')
- new_vector_stat: float32 [13312], P('shard')
Inputs may be any that keep to these rules, and one draw needn't show every extreme that they name: `segments`: taken in order of positions, within each sequence the numbers start at 0 and never fall, rising by at most one from a position to the next; positions 128 to 384 lie in one document, and so do positions 640 to 896. The row of position 0 of every sequence is valid. `left_stat`: every block is symmetric. `right_stat`: every block is symmetric. `left_root`: every block is symmetric. `right_root`: every block is symmetric.
All inputs are finite; a program needn't handle non-finite values.
Results may differ from a plain program's by a relative error of at most 0.012.
Values may be sent and summed in bfloat16 or wider, within the bound.
A program may use at most 320 MiB of HBM per device.

v0:
```python
from functools import partial
import math
import jax
import jax.numpy as jnp
from jax import lax
from jax.sharding import PartitionSpec as P

HD = 64
ROT = 16
BS = 128
EPS = 1e-05
NEG = -1e30
LEARN = 0.5
LEARN_VEC = 0.15
HIGHEST = lax.Precision.HIGHEST


def partner(shard, axis, distance):
    return lax.ppermute(shard, axis, [(i, i ^ 1 << distance) for i in range(lax.axis_size(axis))])


def layer_norm(values, gain, shift):
    row_mean = jnp.mean(values, axis=-1, keepdims=True)
    centred = values - row_mean
    spread = jnp.mean(centred * centred, axis=-1, keepdims=True)
    return centred * lax.rsqrt(spread + EPS) * gain + shift


def rotate(values, cosine_grid, sine_grid):
    half_rot = ROT // 2
    first = values[..., :half_rot]
    second = values[..., half_rot:ROT]
    return jnp.concatenate(
        [
            first * cosine_grid - second * sine_grid,
            second * cosine_grid + first * sine_grid,
            values[..., ROT:],
        ],
        axis=-1,
    )


def angles(positions):
    half_rot = ROT // 2
    frequency = jnp.power(10000.0, -2.0 * jnp.arange(half_rot, dtype=jnp.float32) / ROT)
    angle_grid = positions.astype(jnp.float32)[:, None] * frequency[None, :]
    return (jnp.cos(angle_grid)[:, None, :], jnp.sin(angle_grid)[:, None, :])


def place_rows(parity, row_count):
    half_rows = row_count // 2
    local = jnp.arange(row_count, dtype=jnp.int32)
    block = 2 * parity + local // half_rows
    quarter = jnp.where(block == 0, 0, jnp.where(block == 1, 3, block - 1))
    return quarter * half_rows + local % half_rows


def body(
    tokens,
    targets,
    segments,
    valid,
    master,
    vectors,
    left_stat,
    right_stat,
    left_root,
    right_root,
    vector_stat,
):
    row_count, model_width = tokens.shape
    head_count = model_width // HD
    stack_width = master.shape[1]
    hidden_width = (stack_width - 4 * model_width) // 2
    shard_count = lax.axis_size("shard")
    data_count = lax.axis_size("dp")
    shard_index = lax.axis_index("shard")
    is_later = shard_index % 2
    partner_index = shard_index + 1 - 2 * is_later
    weights, vector_copy = (
        lax.all_gather(master.astype(jnp.bfloat16), "shard", axis=0, tiled=True),
        lax.all_gather(vectors.astype(jnp.bfloat16), "shard", axis=0, tiled=True),
    )
    valid_float = valid.astype(jnp.float32)
    valid_total = lax.psum(jnp.sum(valid_float), ("dp", "shard"))
    params = vector_copy.astype(jnp.float32)
    gain_one = params[0:model_width]
    shift_one = params[model_width : 2 * model_width]
    gain_two = params[2 * model_width : 3 * model_width]
    shift_two = params[3 * model_width : 4 * model_width]
    bias_qkv = params[4 * model_width : 7 * model_width]
    bias_out = params[7 * model_width : 8 * model_width]
    bias_up = params[8 * model_width : 8 * model_width + hidden_width]
    bias_down = params[8 * model_width + hidden_width :]
    w_qkv = weights[:, : 3 * model_width]
    w_out = weights[:, 3 * model_width : 4 * model_width]
    w_up = weights[:, 4 * model_width : 4 * model_width + hidden_width]
    w_down = weights[:, 4 * model_width + hidden_width :]
    inputs = tokens.astype(jnp.float32)
    norm_one, back_one = jax.vjp(layer_norm, inputs, gain_one, shift_one)
    norm_two, back_two = jax.vjp(layer_norm, inputs, gain_two, shift_two)
    one_low = norm_one.astype(jnp.bfloat16)
    two_low = norm_two.astype(jnp.bfloat16)
    projected = jnp.dot(one_low, w_qkv, preferred_element_type=jnp.float32) + bias_qkv
    head_shape = (row_count, head_count, HD)
    positions = place_rows(is_later, row_count)
    partner_pos = place_rows(1 - is_later, row_count)
    cosine_grid, sine_grid = angles(positions)
    turner = partial(rotate, cosine_grid=cosine_grid, sine_grid=sine_grid)
    query_rot, query_back = jax.vjp(turner, projected[:, :model_width].reshape(head_shape))
    key_rot, key_back = jax.vjp(
        turner, projected[:, model_width : 2 * model_width].reshape(head_shape)
    )
    query_low = query_rot.astype(jnp.bfloat16)
    key_low = key_rot.astype(jnp.bfloat16).reshape(row_count, model_width)
    value_low = projected[:, 2 * model_width :].astype(jnp.bfloat16)
    prior_key, prior_value = partner((key_low, value_low), "shard", 0)
    own_ids = lax.dynamic_slice_in_dim(segments, shard_index * row_count, row_count)
    partner_ids = lax.dynamic_slice_in_dim(segments, partner_index * row_count, row_count)
    key_ids = jnp.concatenate([partner_ids, own_ids])
    key_pos = jnp.concatenate([partner_pos, positions])
    allowed = (key_pos[None, :] <= positions[:, None]) & (key_ids[None, :] == own_ids[:, None])
    key_shape = (2 * row_count, head_count, HD)
    key_all = jnp.concatenate([prior_key, key_low], axis=0).reshape(key_shape)
    value_all = jnp.concatenate([prior_value, value_low], axis=0).reshape(key_shape)

    def masked_scores(key_part):
        scores = jnp.einsum(
            "qhe,khe->hqk", query_low, key_part, preferred_element_type=jnp.float32
        ) * HD ** (-0.5)
        return jnp.where(allowed[None], scores, NEG)

    scores = masked_scores(key_all)
    row_max = jnp.max(scores, axis=-1, keepdims=True)
    exponent = jnp.exp(scores - row_max)
    row_sum = jnp.sum(exponent, axis=-1, keepdims=True)
    soft_weights = exponent / row_sum
    attention = jnp.einsum(
        "hqk,khe->qhe",
        soft_weights.astype(jnp.bfloat16),
        value_all,
        preferred_element_type=jnp.float32,
    )
    attention_low = attention.reshape(row_count, model_width).astype(jnp.bfloat16)
    branch = jnp.dot(attention_low, w_out, preferred_element_type=jnp.float32) + bias_out
    up_value = jnp.dot(two_low, w_up, preferred_element_type=jnp.float32) + bias_up
    active, active_back = jax.vjp(partial(jax.nn.gelu, approximate=False), up_value)
    active_low = active.astype(jnp.bfloat16)
    feed_out = (
        jnp.einsum("tf,df->td", active_low, w_down, preferred_element_type=jnp.float32) + bias_down
    )
    outputs = inputs + (branch + feed_out)
    tokens_all = row_count * shard_count * data_count
    grad_out = (
        tokens_all / valid_total * valid_float[:, None] * (outputs - targets.astype(jnp.float32))
    )
    grad_low = grad_out.astype(jnp.bfloat16)
    grad_attention = jnp.einsum("te,de->td", grad_low, w_out, preferred_element_type=jnp.float32)
    grad_attention_low = grad_attention.astype(jnp.bfloat16).reshape(head_shape)
    grad_active = jnp.dot(grad_low, w_down, preferred_element_type=jnp.float32)
    up_low = active_back(grad_active)[0].astype(jnp.bfloat16)
    grad_two = jnp.einsum("tf,df->td", up_low, w_up, preferred_element_type=jnp.float32)
    back_keys, back_values = (key_all, value_all)
    weights_again = jnp.exp(masked_scores(back_keys) - row_max) / row_sum
    grad_weights = jnp.einsum(
        "qhe,khe->hqk", grad_attention_low, back_values, preferred_element_type=jnp.float32
    )
    weighted_sum = jnp.sum(weights_again * grad_weights, axis=-1, keepdims=True)
    grad_scores = (weights_again * (grad_weights - weighted_sum)).astype(jnp.bfloat16)
    grad_query = jnp.einsum(
        "hqk,khe->qhe", grad_scores, back_keys, preferred_element_type=jnp.float32
    ) * HD ** (-0.5)
    grad_keys = jnp.einsum(
        "hqk,qhe->khe", grad_scores, query_low, preferred_element_type=jnp.float32
    ) * HD ** (-0.5)
    grad_values = jnp.einsum(
        "hqk,qhe->khe",
        weights_again.astype(jnp.bfloat16),
        grad_attention_low,
        preferred_element_type=jnp.float32,
    )
    back_key, back_value = (
        partner(
            grad_keys[:row_count].reshape(row_count, model_width).astype(jnp.bfloat16), "shard", 0
        ).astype(jnp.float32),
        partner(
            grad_values[:row_count].reshape(row_count, model_width).astype(jnp.bfloat16), "shard", 0
        ).astype(jnp.float32),
    )
    own_key_grad = grad_keys[row_count:].reshape(row_count, model_width) + back_key
    own_value_grad = grad_values[row_count:].reshape(row_count, model_width) + back_value
    query_pre = query_back(grad_query)[0].reshape(row_count, model_width)
    key_pre = key_back(own_key_grad.reshape(head_shape))[0].reshape(row_count, model_width)
    qkv_low = jnp.concatenate([query_pre, key_pre, own_value_grad], axis=1).astype(jnp.bfloat16)
    grad_one = jnp.einsum("tc,dc->td", qkv_low, w_qkv, preferred_element_type=jnp.float32)
    input_one, gain_one_grad, shift_one_grad = back_one(grad_one)
    input_two, gain_two_grad, shift_two_grad = back_two(grad_two)
    input_grad = grad_out + input_one + input_two
    grad_low_sum = jnp.sum(grad_low.astype(jnp.float32), axis=0)
    vector_grad = jnp.concatenate(
        [
            gain_one_grad,
            shift_one_grad,
            gain_two_grad,
            shift_two_grad,
            jnp.sum(qkv_low.astype(jnp.float32), axis=0),
            grad_low_sum,
            jnp.sum(up_low.astype(jnp.float32), axis=0),
            grad_low_sum,
        ]
    )
    weight_grad = jnp.concatenate(
        [
            jnp.einsum("td,tc->dc", one_low, qkv_low, preferred_element_type=jnp.float32),
            jnp.einsum("td,te->de", attention_low, grad_low, preferred_element_type=jnp.float32),
            jnp.einsum("td,tf->df", two_low, up_low, preferred_element_type=jnp.float32),
            jnp.einsum("te,tf->ef", grad_low, active_low, preferred_element_type=jnp.float32),
        ],
        axis=1,
    )
    spread_vec = vector_grad.reshape(shard_count, data_count, -1).transpose(1, 0, 2).reshape(-1)
    part_weight, part_vector = (
        lax.psum_scatter(weight_grad, "dp", scatter_dimension=1, tiled=True),
        lax.psum_scatter(spread_vec, "dp", scatter_dimension=0, tiled=True),
    )
    part_weight, part_vector = (
        lax.psum_scatter(part_weight, "shard", scatter_dimension=0, tiled=True),
        lax.psum_scatter(part_vector, "shard", scatter_dimension=0, tiled=True),
    )
    own_weight, own_vector = (
        lax.all_gather(part_weight, "dp", axis=1, tiled=True),
        lax.all_gather(part_vector, "dp", axis=0, tiled=True),
    )
    square_sum = jnp.sum(own_weight * own_weight) + jnp.sum(own_vector * own_vector)
    grad_norm = jnp.sqrt(lax.psum(square_sum, "shard"))
    factor = jnp.minimum(1.0, math.sqrt(model_width * stack_width / BS) / grad_norm)
    own_rows = own_weight.shape[0]
    tiles = (own_weight * factor).reshape(own_rows // BS, BS, stack_width // BS, BS)
    new_left = 0.5 * left_stat + 0.5 * jnp.einsum(
        "iajb,icjb->ijac", tiles, tiles, precision=HIGHEST
    )
    new_right = 0.5 * right_stat + 0.5 * jnp.einsum(
        "iajb,iajd->ijbd", tiles, tiles, precision=HIGHEST
    )
    tiles_low = tiles.astype(jnp.bfloat16)
    left_mixed = jnp.einsum(
        "ijac,icjd->iajd", left_root, tiles_low, preferred_element_type=jnp.float32
    ).astype(jnp.bfloat16)
    update = jnp.einsum(
        "iajd,ijdb->iajb", left_mixed, right_root, preferred_element_type=jnp.float32
    ).reshape(own_rows, stack_width)
    new_master = master - LEARN * update
    scaled_vec = own_vector * factor
    new_vstat = 0.5 * vector_stat + 0.5 * scaled_vec * scaled_vec
    new_vectors = vectors - LEARN_VEC * scaled_vec / jnp.sqrt(new_vstat)
    return (
        input_grad,
        grad_norm,
        new_left,
        new_right,
        new_master,
        new_master.astype(jnp.bfloat16),
        new_vectors,
        new_vstat,
    )


def solution(mesh):
    return jax.shard_map(
        body,
        mesh=mesh,
        in_specs=(
            P(("dp", "shard"), None),
            P(("dp", "shard"), None),
            P("dp"),
            P(("dp", "shard")),
            P("shard", None),
            P("shard"),
            P("shard", None, None, None),
            P("shard", None, None, None),
            P("shard", None, None, None),
            P("shard", None, None, None),
            P("shard"),
        ),
        out_specs=(
            P(("dp", "shard"), None),
            P(),
            P("shard", None, None, None),
            P("shard", None, None, None),
            P("shard", None),
            P("shard", None),
            P("shard"),
            P("shard"),
        ),
        check_vma=False,
    )
```

profile of v0, /device:TPU:0, one launch (start us, length us, event | category | flops | bytes accessed | tf_op | source)
XLA Modules:
  0.0 1619.4 jit_solution(14062656077153369523)
XLA Ops:
  7.3 5.0 convert_element_type.116
  12.9 42.6 %psum.14 = f32[]{:T(128)} all-reduce(f32[]{:T(128)} %convert_reduce_fusion.4), channel_id=1, replica_groups=mesh['dp'=4,'shard'=8] {'dp','shard'}, use_global_device_ids=true, to_apply=%region_1.2 | all-reduce | flops 1 | bytes 8 | tf_op jit(solution)/shard_map/psum | solution.py:85
  55.6 10.1 all-gather
  67.4 1.4 convert_reduce_fusion.2
  68.8 2.0 fusion.86
  72.7 1.3 compare_and_fusion
  74.0 67.4 %all-gather.4.cloned.1.call-done = bf16[1024,12288]{1,0:T(8,128)(2,1)} async-done(((bf16[128,12288]{1,0:T(8,128)(2,1)}), bf16[1024,12288]{1,0:T(8,128)(2,1)}) %all-gather.4.cloned.1.call-update) | async-done | bytes 25165840 | tf_op jit(solution)/shard_map/all_gather | solution.py:81
  141.4 6.1 fusion.35
  147.5 1.1 slice.167
  148.7 2.5 fusion.135
  151.5 2.9 copy.67
  154.4 1.5 slice.116
  155.9 1.1 multiply_subtract_fusion
  157.0 1.1 maximum_convert_fusion
  158.4 26.6 %multiply_convert_fusion.1 = (bf16[512,4096]{1,0:T(8,128)(2,1)}, f32[512,4096]{1,0:T(8,128)}, f32[512,4096]{1,0:T(8,128)}) fusion(f32[4096]{0:T(1024)S(1)} %slice.122, bf16[1024,12288]{1,0:T(8,128)(2,1)} %all-gather.4.cloned.1.call-done, bf16[512,1024]{1,0:T(8,128)(2,1)} %param.11, f32[1024]{0:T(1024)S(1)} %get-tuple-element.42, ...), kind=kOutput, calls=%fused_computation.15 | convolution fusion | flops 4436525056 | bytes 30437376 | tf_op jit(solution)/shard_map/dot_general | solution.py:146
  185.0 2.9 copy.66
  187.9 2.4 slice.168
  191.5 3.1 pad_maximum_fusion.2
  194.6 4.1 copy.65
  198.7 17.4 %fusion.104 = f32[16,512,1024]{2,1,0:T(8,128)} fusion(bf16[512,16,64]{0,2,1:T(8,128)(2,1)} %maximum_convert_fusion, bf16[512,16,64]{0,2,1:T(8,128)(2,1)} %bitcast.5, bf16[512,16,48]{0,2,1:T(8,128)(2,1)} %slice.168, bf16[512,16,8]{0,2,1:T(8,128)(2,1)S(1)} %get-tuple-element.35, bf16[512,16,8]{0,2,1:T(8,128)(2,1)S(1)} %get-tuple-element.34), kind=kOutput, calls=%fused_computation.119 | convolution fusion | flops 1081081856 | bytes 36700160 | tf_op jit(solution)/shard_map/qhe,khe->hqk/dot_general | solution.py:128
  216.1 38.1 %fusion.139 = (f32[16,512]{1,0:T(8,128)S(1)}, f32[16,512,1024]{2,1,0:T(8,128)}) fusion(f32[16,512,1024]{2,1,0:T(8,128)} %fusion.104, pred[512,1024]{1,0:T(8,128)(4,1)} %compare_and_fusion), kind=kOutput, calls=%fused_computation.189 | output fusion | flops 50332672 | bytes 67665920 | tf_op jit(solution)/shard_map/sub | solution.py:135
  254.2 15.2 fusion.98
  269.4 3.2 fusion.94
  272.6 12.1 convert_reduce_fusion.3
  285.7 3.9 fusion.101
  289.6 2.3 copy.68
  291.9 14.9 fusion.75
  306.9 22.4 %multiply_reduce_fusion = (f32[16,512]{1,0:T(8,128)S(1)}, f32[16,512,1024]{2,1,0:T(8,128)}) fusion(f32[16,512,1024]{2,1,0:T(8,128)} %get-tuple-element.57, f32[16,512]{1,0:T(8,128)S(1)} %get-tuple-element.56, bf16[512,16,64]{0,2,1:T(8,128)(2,1)S(1)} %bitcast.119, bf16[1024,16,64]{0,2,1:T(8,128)(2,1)S(1)} %bitcast.115), kind=kOutput, calls=%fused_computation.3 | convolution fusion | flops 1098899456 | bytes 70320128 | tf_op jit(solution)/shard_map/qhe,khe->hqk/dot_general | solution.py:165
  329.3 8.1 fusion.141
  337.5 1.1 slice.165
  338.9 28.0 %multiply_convert_fusion = bf16[16,512,1024]{2,1,0:T(8,128)(2,1)} fusion(f32[16,512,1024]{2,1,0:T(8,128)} %get-tuple-element.61, f32[16,512]{1,0:T(8,128)S(1)} %get-tuple-element.60, f32[16,512,1024]{2,1,0:T(8,128)} %get-tuple-element.57, f32[16,512]{1,0:T(8,128)S(1)} %get-tuple-element.56), kind=kLoop, calls=%fused_computation.2 | loop fusion | flops 33554432 | bytes 83951616 | tf_op jit(solution)/shard_map/convert_element_type | solution.py:169
  366.9 9.1 multiply_bitcast_fusion.2
  376.0 1.3 slice.166
  378.4 13.2 convert_reduce_fusion
  391.6 2.0 copy-done.56
  393.6 8.6 fusion.122
  402.2 12.9 multiply_bitcast_fusion.3
  415.2 4.9 fusion.140
  420.1 2.2 slice-done
  422.3 1.7 bitcast_add_fusion.3
  424.8 1.9 slice-done.2
  426.7 1.7 fusion.91
  429.4 9.8 fusion.125
  439.2 33.4 %pad_maximum_fusion = f32[1024,12288]{1,0:T(8,128)} fusion(f32[1024,4096]{1,0:T(8,128)} %fusion.141, f32[1024,4096]{1,0:T(8,128)} %fusion.122, f32[1024,1024]{1,0:T(8,128)} %fusion.140, f32[1024,3072]{1,0:T(8,128)} %fusion.125), kind=kLoop, calls=%fused_computation.1 | loop fusion | flops 37748736 | bytes 100663296 | tf_op jit(solution)/shard_map/concatenate | solution.py:212
  472.7 820.8 %reduce-scatter.3.cloned.1.call-done = f32[1024,3072]{1,0:T(8,128)} async-done(((f32[1024,12288]{1,0:T(8,128)}), f32[1024,3072]{1,0:T(8,128)}) %reduce-scatter.3.cloned.1.call-update) | async-done | bytes 12582928 | tf_op jit(solution)/shard_map/reduce_scatter | solution.py:223
  1293.6 98.3 %reduce-scatter.5.cloned.1.call-done = f32[128,3072]{1,0:T(8,128)} async-done(((f32[1024,3072]{1,0:T(8,128)}), f32[128,3072]{1,0:T(8,128)}) %reduce-scatter.5.cloned.1.call-update) | async-done | bytes 1572880 | tf_op jit(solution)/shard_map/reduce_scatter | solution.py:227
  1395.1 8.6 fusion.19
  1403.7 7.9 fusion.131
  1411.7 2.0 fusion.85
  1415.1 21.5 %all-reduce.7 = f32[13312]{0:T(1024)S(1)} all-reduce(f32[13312]{0:T(1024)S(1)} %reshape.306), channel_id=4, replica_groups=mesh['dp'=4,'shard'=8] {'dp'}, use_global_device_ids=true, to_apply=%region_21.22.clone | all-reduce | flops 13312 | bytes 106496
  1436.7 25.6 %all-reduce.8 = f32[3328]{0:T(1024)S(1)} all-reduce(f32[3328]{0:T(1024)S(1)} %dynamic-slice.2), channel_id=5, replica_groups=mesh['dp'=4,'shard'=8] {'shard'}, use_global_device_ids=true, to_apply=%region_22.23.clone | all-reduce | flops 3328 | bytes 26624
  1462.4 11.3 all-reduce.6
  1474.3 37.0 %all-gather.6.cloned.1.call-done = f32[128,12288]{1,0:T(8,128)} async-done(((f32[128,3072]{1,0:T(8,128)}), f32[128,12288]{1,0:T(8,128)}) %all-gather.6.cloned.1.call-update) | async-done | bytes 6291472 | tf_op jit(solution)/shard_map/all_gather | solution.py:231
  1511.3 5.0 multiply_reduce_fusion.1
  1517.6 4.8 add_add_fusion.2
  1522.4 14.7 psum.15
  1537.8 6.6 multiply_bitcast_fusion.1
  1544.4 3.8 copy.83
  1548.2 6.6 copy.73
  1554.8 18.9 %fusion.28 = f32[1,96,128,128]{3,2,1,0:T(8,128)} fusion(f32[1,96,128,128]{3,2,1,0:T(8,128)} %param.17, f32[16,96,8,128]{3,2,1,0:T(8,128)} %get-tuple-element.27), kind=kOutput, calls=%fused_computation.48 | convolution fusion | flops 2419064832 | bytes 18874368 | tf_op jit(solution)/shard_map/iajb,icjb->ijac/dot_general | solution.py:239
  1573.7 11.6 fusion.27
  1585.3 9.7 broadcast_multiply_fusion
  1595.0 6.6 copy.78
  1601.6 9.3 fusion.133
  (177 shorter events, 13.3 us)
Async XLA Ops:
  7.2 1578.1 %copy-start = (bf16[1,96,128,128]{3,2,1,0:T(8,128)(2,1)S(1)}, bf16[1,96,128,128]{3,2,1,0:T(8,128)(2,1)}, u32[]{:S(2)}) copy-start(bf16[1,96,128,128]{3,2,1,0:T(8,128)(2,1)} %param.20) | copy-start | bytes 9437188
  7.2 5.1 copy-start.45
  7.2 48.3 %copy-start.36 = (f32[1664]{0:T(1024)S(1)}, f32[1664]{0:T(1024)}, u32[]{:S(2)}) copy-start(f32[1664]{0:T(1024)} %param.16) | copy-start | bytes 19972
  7.2 134.2 %all-gather.4.cloned.1.call-start = ((), (), s32[]{:S(2)}) async-start(), calls=%async_computation.2 | async-start | bytes 28311552 | tf_op jit(solution)/shard_map/all_gather | solution.py:81
  12.3 1281.2 %reduce-scatter.3.cloned.1.call-start = ((), (), s32[]{:S(2)}) async-start(), calls=%async_computation.3 | async-start | bytes 62914560 | tf_op jit(solution)/shard_map/reduce_scatter | solution.py:223
  65.7 92.6 %copy-start.42 = (f32[4096]{0:T(1024)}, f32[4096]{0:T(1024)S(1)}, u32[]{:S(2)}) copy-start(f32[4096]{0:T(1024)S(1)} %slice.122) | copy-start | bytes 49156
  68.8 89.6 %copy-start.34 = (f32[512]{0:T(512)}, f32[512]{0:T(512)S(1)}, u32[]{:S(2)}) copy-start(f32[512]{0:T(512)S(1)} %broadcast_multiply_fusion.1) | copy-start | bytes 6148
  71.4 87.0 %copy-start.38 = (f32[512]{0:T(512)}, f32[512]{0:T(512)S(1)}, u32[]{:S(2)}) copy-start(f32[512]{0:T(512)S(1)} %fusion.115) | copy-start | bytes 6148
  72.6 75.0 %copy-start.32 = (f32[1024]{0:T(1024)}, f32[1024]{0:T(1024)S(1)}, u32[]{:S(2)}) copy-start(f32[1024]{0:T(1024)S(1)} %get-tuple-element.45) | copy-start | bytes 12292
  72.6 75.0 %copy-start.47 = (f32[1024]{0:T(1024)}, f32[1024]{0:T(1024)S(1)}, u32[]{:S(2)}) copy-start(f32[1024]{0:T(1024)S(1)} %get-tuple-element.44) | copy-start | bytes 12292
  72.6 85.8 %copy-start.30 = (f32[1024]{0:T(1024)}, f32[1024]{0:T(1024)S(1)}, u32[]{:S(2)}) copy-start(f32[1024]{0:T(1024)S(1)} %get-tuple-element.43) | copy-start | bytes 12292
  72.6 85.8 %copy-start.49 = (f32[1024]{0:T(1024)}, f32[1024]{0:T(1024)S(1)}, u32[]{:S(2)}) copy-start(f32[1024]{0:T(1024)S(1)} %get-tuple-element.42) | copy-start | bytes 12292
  72.7 117.6 %copy-start.26 = (f32[512,8]{0,1:T(8,128)}, f32[512,8]{0,1:T(8,128)S(1)}, u32[]{:S(2)}) copy-start(f32[512,8]{0,1:T(8,128)S(1)} %get-tuple-element.50) | copy-start | bytes 49156
  72.7 117.6 %copy-start.28 = (f32[512,8]{0,1:T(8,128)}, f32[512,8]{0,1:T(8,128)S(1)}, u32[]{:S(2)}) copy-start(f32[512,8]{0,1:T(8,128)S(1)} %get-tuple-element.51) | copy-start | bytes 49156
  151.2 40.2 %collective-permute-start = (bf16[512,1024]{1,0:T(8,128)(2,1)}, bf16[512,1024]{1,0:T(8,128)(2,1)}, u32[]{:S(2)}, u32[]{:S(2)}) collective-permute-start(bf16[512,1024]{1,0:T(8,128)(2,1)} %slice.167), channel_id=1, source_target_pairs={{0,1},{1,0},{2,3},{3,2},{4,5},{5,4},{6,7},{7,6},{8,9},{9,8},{10,11... | collective-permute-start | bytes 3145736 | tf_op jit(solution)/shard_map/ppermute | solution.py:19
  158.1 40.5 %collective-permute-start.1 = (bf16[512,1024]{0,1:T(8,128)(2,1)}, bf16[512,1024]{0,1:T(8,128)(2,1)}, u32[]{:S(2)}, u32[]{:S(2)}) collective-permute-start(bf16[512,1024]{0,1:T(8,128)(2,1)} %bitcast.4), channel_id=1, source_target_pairs={{0,1},{1,0},{2,3},{3,2},{4,5},{5,4},{6,7},{7,6},{8,9},{9,8},{10,11... | collective-permute-start | bytes 3145736 | tf_op jit(solution)/shard_map/ppermute | solution.py:19
  191.4 24.6 %copy-start.18 = (bf16[512,16,8]{0,2,1:T(8,128)(2,1)}, bf16[512,16,8]{0,2,1:T(8,128)(2,1)S(1)}, u32[]{:S(2)}) copy-start(bf16[512,16,8]{0,2,1:T(8,128)(2,1)S(1)} %get-tuple-element.34) | copy-start | bytes 393220
  191.4 24.6 %copy-start.20 = (bf16[512,16,8]{0,2,1:T(8,128)(2,1)}, bf16[512,16,8]{0,2,1:T(8,128)(2,1)S(1)}, u32[]{:S(2)}) copy-start(bf16[512,16,8]{0,2,1:T(8,128)(2,1)S(1)} %get-tuple-element.35) | copy-start | bytes 393220
  254.2 18.4 %copy-start.51 = (f32[1024]{0:T(1024)S(1)}, f32[1024]{0:T(1024)}, u32[]{:S(2)}) copy-start(f32[1024]{0:T(1024)} %get-tuple-element.40) | copy-start | bytes 12292
  254.2 18.4 %copy-start.52 = (f32[1024]{0:T(1024)S(1)}, f32[1024]{0:T(1024)}, u32[]{:S(2)}) copy-start(f32[1024]{0:T(1024)} %get-tuple-element.41) | copy-start | bytes 12292
  254.2 18.4 %copy-start.54 = (f32[512]{0:T(512)S(1)}, f32[512]{0:T(512)}, u32[]{:S(2)}) copy-start(f32[512]{0:T(512)} %convert_multiply_fusion) | copy-start | bytes 6148
  291.9 14.9 copy-start.17
  291.9 14.9 copy-start.22
  306.8 22.5 %copy-start.16 = (bf16[512,4096]{1,0:T(8,128)(2,1)S(1)}, bf16[512,4096]{1,0:T(8,128)(2,1)}, u32[]{:S(2)}) copy-start(bf16[512,4096]{1,0:T(8,128)(2,1)} %get-tuple-element.24) | copy-start | bytes 12582916
  306.9 22.5 %copy-start.24 = (bf16[512,1024]{1,0:T(8,128)(2,1)S(1)}, bf16[512,1024]{1,0:T(8,128)(2,1)}, u32[]{:S(2)}) copy-start(bf16[512,1024]{1,0:T(8,128)(2,1)} %copy-done.23) | copy-start | bytes 3145732
  329.3 8.2 copy-start.7
  338.6 86.2 %collective-permute-start.3 = (bf16[512,1024]{0,1:T(8,128)(2,1)}, bf16[512,1024]{0,1:T(8,128)(2,1)}, u32[]{:S(2)}, u32[]{:S(2)}) collective-permute-start(bf16[512,1024]{0,1:T(8,128)(2,1)} %bitcast.18), channel_id=1, source_target_pairs={{0,1},{1,0},{2,3},{3,2},{4,5},{5,4},{6,7},{7,6},{8,9},{9,8},{10,11... | collective-permute-start | bytes 3145736 | tf_op jit(solution)/shard_map/ppermute | solution.py:19
  338.9 28.0 %copy-start.19 = (bf16[512,16,8]{0,2,1:T(8,128)(2,1)S(1)}, bf16[512,16,8]{0,2,1:T(8,128)(2,1)}, u32[]{:S(2)}) copy-start(bf16[512,16,8]{0,2,1:T(8,128)(2,1)} %copy-done.18) | copy-start | bytes 393220
  338.9 28.0 %copy-start.21 = (bf16[512,16,8]{0,2,1:T(8,128)(2,1)S(1)}, bf16[512,16,8]{0,2,1:T(8,128)(2,1)}, u32[]{:S(2)}) copy-start(bf16[512,16,8]{0,2,1:T(8,128)(2,1)} %copy-done.20) | copy-start | bytes 393220
  366.8 11.5 copy-start.25
  366.9 11.5 copy-start.43
  376.0 2.3 copy-start.5
  377.3 42.8 %collective-permute-start.2 = (bf16[512,1024]{0,1:T(8,128)(2,1)}, bf16[512,1024]{0,1:T(8,128)(2,1)}, u32[]{:S(2)}, u32[]{:S(2)}) collective-permute-start(bf16[512,1024]{0,1:T(8,128)(2,1)} %bitcast.13), channel_id=1, source_target_pairs={{0,1},{1,0},{2,3},{3,2},{4,5},{5,4},{6,7},{7,6},{8,9},{9,8},{10,11... | collective-permute-start | bytes 3145736 | tf_op jit(solution)/shard_map/ppermute | solution.py:19
  378.3 15.2 copy-start.2
  378.3 15.2 copy-start.31
  378.3 15.2 copy-start.35
  378.3 15.2 copy-start.39
  378.4 15.2 copy-start.50
  420.1 2.3 slice-start
  420.1 4.2 copy-start.6
  420.1 4.2 copy-start.27
  420.1 4.2 copy-start.29
  420.1 4.6 slice-start.1
  424.1 2.7 slice-start.2
  424.3 5.2 copy-start.3
  424.3 5.2 copy-start.33
  424.3 5.2 copy-start.48
  424.6 3.8 copy-start.10
  424.8 3.7 copy-start.12
  472.7 919.2 %reduce-scatter.5.cloned.1.call-start = ((), (), s32[]{:S(2)}) async-start(), calls=%async_computation.4 | async-start | bytes 14155776 | tf_op jit(solution)/shard_map/reduce_scatter | solution.py:227
  1293.5 98.4 %copy-start.55 = (u32[32]{0:T(128)S(1)}, u32[32]{0:T(128)}, u32[]{:S(2)}) copy-start(u32[32]{0:T(128)} %constant.199) | copy-start | bytes 388
  1293.5 99.0 %copy-start.53 = (u32[32]{0:T(128)S(1)}, u32[32]{0:T(128)}, u32[]{:S(2)}) copy-start(u32[32]{0:T(128)} %constant.189) | copy-start | bytes 388
  1293.5 217.8 %all-gather.6.cloned.1.call-start = ((), (), s32[]{:S(2)}) async-start(), calls=%async_computation.5 | async-start | bytes 7864320 | tf_op jit(solution)/shard_map/all_gather | solution.py:231
  1395.1 8.6 copy-start.4
  1395.1 8.6 copy-start.11
  1395.1 8.6 copy-start.13
  1395.1 8.6 copy-start.15
  1403.7 8.0 copy-start.8
  1403.7 8.0 copy-start.41
  1411.7 2.0 copy-start.9
  1411.7 3.1 copy-start.44
  1554.8 18.9 %copy-start.1 = (f32[128,96,128]{0,2,1:T(8,128)S(1)}, f32[128,96,128]{0,2,1:T(8,128)}, u32[]{:S(2)}) copy-start(f32[128,96,128]{0,2,1:T(8,128)} %copy.73) | copy-start | bytes 18874372
  1601.6 9.3 copy-start.37
  1601.6 9.3 copy-start.46
  (4 other events, 4.6 us)
Sparse Core Ops, SparseCore 0:
  12.4 129.0 all-gather.3
  472.8 820.6 reduce-scatter.2
  1297.4 94.4 reduce-scatter.4
  1393.4 117.8 all-gather.5
where the time goes:
time: 1630 us; the launch traced here: 1620 us
  waiting for transfers between devices  1020 us (63%)
  matrix products  245 us (15%)
  other arithmetic  151 us (9%)
  blocking collectives  126 us (8%)
  local copies, waits for them, and re-layouts  52.1 us (3%)
  between operations  20.6 us (1%)
    reduce_scatter x1, waiting for transfers between devices, body(): lax.psum_scatter(weight_grad, 'dp', scatter_dimension=1, tiled=True)  821 us
    reduce_scatter x1, waiting for transfers between devices, body(): lax.psum_scatter(part_weight, 'shard', scatter_dimension=0, tiled=True)  98.3 us
    all_gather x1, waiting for transfers between devices, body(): lax.all_gather(master.astype(jnp.bfloat16), 'shard', axis=0, tiled=True)  67.4 us
    unnamed x3, blocking collectives  58.4 us
    psum x1, blocking collectives, body(): valid_total = lax.psum(jnp.sum(valid_float), ('dp', 'shard'))  42.6 us
    sub x1, other arithmetic, body(): exponent = jnp.exp(scores - row_max)  38.1 us
    all_gather x1, waiting for transfers between devices, body(): lax.all_gather(part_weight, 'dp', axis=1, tiled=True)  37 us
    concatenate x1, other arithmetic, body(): jnp.concatenate([jnp.einsum('td,tc->dc', one_low, qkv_low, preferred_elem...  33.4 us
  transfers between devices with their start and end apart: 8, of which 4 were waited for; matrix products, arithmetic and copies ran while one was open for 10% of the time, Pallas kernels for 0%

commit v1 on v0

--- a/solution.py
+++ b/solution.py
@@ -13,6 +13,28 @@
 LEARN = 0.5
 LEARN_VEC = 0.15
 HIGHEST = lax.Precision.HIGHEST
+
+
+def in_order(pieces, dim):
+    dims = list(pieces.shape[1:])
+    dims[dim] *= pieces.shape[0]
+    return jnp.moveaxis(pieces, 0, dim).reshape(dims)
+
+
+def collected_by_bits(array, axis):
+    size = lax.axis_size(axis)
+    tiles = array[None]
+    for level in range(size.bit_length() - 1):
+        distance = 1 << level
+        other = lax.ppermute(tiles, axis, [(i, i ^ distance) for i in range(size)])
+        both = jnp.stack([tiles, other])
+        upper = lax.axis_index(axis) >> level & 1
+        tiles = jnp.where(upper == 0, both, both[::-1]).reshape(-1, *array.shape)
+    return tiles
+
+
+def collect(x, axis, dim):
+    return in_order(collected_by_bits(x, axis), dim)
 
 
 def partner(shard, axis, distance):
@@ -78,7 +100,7 @@
     is_later = shard_index % 2
     partner_index = shard_index + 1 - 2 * is_later
     weights, vector_copy = (
-        lax.all_gather(master.astype(jnp.bfloat16), "shard", axis=0, tiled=True),
+        collect(master.astype(jnp.bfloat16), "shard", 0),
         lax.all_gather(vectors.astype(jnp.bfloat16), "shard", axis=0, tiled=True),
     )
     valid_float = valid.astype(jnp.float32)

time: 1630 us -> 2020 us (1.24)
  blocking collectives: 126 us -> 387 us
  waiting for transfers between devices: 1020 us -> 1100 us
  other arithmetic: 151 us -> 210 us
    psum x1, blocking collectives: 42.6 us -> 304 us  [body(): valid_total = lax.psum(jnp.sum(valid_float), ('dp', 'shard'))]
    ppermute x0 -> x3, waiting for transfers between devices: none -> 142 us  [collected_by_bits(): other = lax.ppermute(tiles, axis, [(i, i ^ distance) for i in range(size)])]
    all_gather x1 -> x0, waiting for transfers between devices: 67.4 us -> none  [body(): lax.all_gather(master.astype(jnp.bfloat16), 'shard', axis=0, tiled=True)]
    another operation x4 -> x9, other arithmetic: 3.13 us -> 46.1 us  [the longest x5 42.9 us: collected_by_bits(): both = jnp.stack([tiles, other])]
    select_n x0 -> x2, other arithmetic: none -> 21.4 us  [collected_by_bits(): tiles = jnp.where(upper == 0, both, both[::-1]).reshape(-1, *array.shape)]
  transfers between devices with their start and end apart: 8 -> 10, of which waited for: 4 -> 5; matrix products, arithmetic and copies ran while one was open for 10% -> 8% of each run, Pallas kernels for 0% -> 0%
where the time goes in v1:
time: 2020 us
  waiting for transfers between devices  1100 us (54%)
  blocking collectives  387 us (19%)
  matrix products  246 us (12%)
  other arithmetic  210 us (10%)
  local copies, waits for them, and re-layouts  52.1 us (3%)
  between operations  20.7 us (1%)
    reduce_scatter x1, waiting for transfers between devices, body(): lax.psum_scatter(weight_grad, 'dp', scatter_dimension=1, tiled=True)  819 us
    psum x1, blocking collectives, body(): valid_total = lax.psum(jnp.sum(valid_float), ('dp', 'shard'))  304 us
    ppermute x3, waiting for transfers between devices, collected_by_bits(): other = lax.ppermute(tiles, axis, [(i, i ^ distance) for i in range(size)])  142 us
    reduce_scatter x1, waiting for transfers between devices, body(): lax.psum_scatter(part_weight, 'shard', scatter_dimension=0, tiled=True)  98.3 us
    unnamed x3, blocking collectives  58.3 us
    another operation x5, other arithmetic, collected_by_bits(): both = jnp.stack([tiles, other])  42.9 us
  transfers between devices with their start and end apart: 10, of which 5 were waited for; matrix products, arithmetic and copies ran while one was open for 8% of the time, Pallas kernels for 0%

profile of v1, /device:TPU:0, one launch (start us, length us, event | category | flops | bytes accessed | tf_op | source)
XLA Modules:
  0.0 2017.5 jit_solution(4784482321051394474)
XLA Ops:
  7.2 6.4 convert_bitcast_fusion.1
  14.1 5.6 collective-permute-done
  19.7 6.1 pad_maximum_fusion.3
  25.9 12.3 fusion.36
  38.2 2.9 collective-permute-start.1
  41.0 136.1 %collective-permute-done.1 = bf16[2,128,12288]{2,1,0:T(8,128)(2,1)} collective-permute-done((bf16[2,128,12288]{2,1,0:T(8,128)(2,1)}, bf16[2,128,12288]{2,1,0:T(8,128)(2,1)}, u32[]{:S(2)}, u32[]{:S(2)}) %collective-permute-start.1) | collective-permute-done | bytes 6291488 | tf_op jit(solution)/shard_map/ppermute | solution.py:29
  177.2 6.1 pad_maximum_fusion.2
  183.3 7.4 reverse_select_fusion.1
  190.7 1.8 collective-permute-start.2
  193.1 304.2 %psum.14 = f32[]{:T(128)} all-reduce(f32[]{:T(128)} %convert_reduce_fusion.4), channel_id=1, replica_groups=mesh['dp'=4,'shard'=8] {'dp','shard'}, use_global_device_ids=true, to_apply=%region_1.2 | all-reduce | flops 1 | bytes 8 | tf_op jit(solution)/shard_map/psum | solution.py:107
  497.3 10.1 all-gather
  515.4 11.9 pad_maximum_fusion.1
  527.4 14.0 reverse_select_fusion
  541.4 5.8 fusion.37
  548.4 2.5 fusion.137
  551.2 2.9 copy.67
  558.1 26.6 %multiply_convert_fusion.1 = (bf16[512,4096]{1,0:T(8,128)(2,1)}, f32[512,4096]{1,0:T(8,128)}, f32[512,4096]{1,0:T(8,128)}) fusion(f32[4096]{0:T(1024)S(1)} %slice.122, bf16[1024,12288]{1,0:T(8,128)(2,1)} %bitcast.115, bf16[512,1024]{1,0:T(8,128)(2,1)} %param.11, f32[1024]{0:T(1024)S(1)} %get-tuple-element.46, f32[1024]{0:T(1024)S(1)} %get-tuple-element.47, ...), kind=kOutput, calls=%fused_computation.20 | convolution fusion | flops 4436525056 | bytes 30437376 | tf_op jit(solution)/shard_map/dot_general | solution.py:168
  584.7 2.9 copy.66
  587.6 2.4 slice.168
  591.1 3.1 pad_maximum_fusion.5
  594.3 4.1 copy.65
  598.4 17.4 fusion.106
  615.8 38.2 %fusion.141 = (f32[16,512]{1,0:T(8,128)S(1)}, f32[16,512,1024]{2,1,0:T(8,128)}) fusion(f32[16,512,1024]{2,1,0:T(8,128)} %fusion.106, pred[512,1024]{1,0:T(8,128)(4,1)} %compare_and_fusion), kind=kOutput, calls=%fused_computation.199 | output fusion | flops 50332672 | bytes 67665920 | tf_op jit(solution)/shard_map/sub | solution.py:157
  654.0 15.4 fusion.100
  669.4 3.2 fusion.96
  672.6 12.2 convert_reduce_fusion.3
  685.8 3.9 fusion.103
  689.7 2.3 copy.68
  692.0 14.9 fusion.77
  706.9 22.4 %multiply_reduce_fusion = (f32[16,512]{1,0:T(8,128)S(1)}, f32[16,512,1024]{2,1,0:T(8,128)}) fusion(f32[16,512,1024]{2,1,0:T(8,128)} %get-tuple-element.61, f32[16,512]{1,0:T(8,128)S(1)} %get-tuple-element.60, bf16[512,16,64]{0,2,1:T(8,128)(2,1)S(1)} %bitcast.141, bf16[1024,16,64]{0,2,1:T(8,128)(2,1)S(1)} %bitcast.137), kind=kOutput, calls=%fused_computation.4 | convolution fusion | flops 1098899456 | bytes 70320128 | tf_op jit(solution)/shard_map/qhe,khe->hqk/dot_general | solution.py:187
  729.4 8.2 fusion.143
  739.1 27.7 %multiply_convert_fusion = bf16[16,512,1024]{2,1,0:T(8,128)(2,1)} fusion(f32[16,512,1024]{2,1,0:T(8,128)} %get-tuple-element.65, f32[16,512]{1,0:T(8,128)S(1)} %get-tuple-element.64, f32[16,512,1024]{2,1,0:T(8,128)} %get-tuple-element.61, f32[16,512]{1,0:T(8,128)S(1)} %get-tuple-element.60), kind=kLoop, calls=%fused_computation.3 | loop fusion | flops 33554432 | bytes 83951616 | tf_op jit(solution)/shard_map/convert_element_type | solution.py:191
  766.9 9.1 multiply_bitcast_fusion.2
  778.4 13.2 convert_reduce_fusion
  791.6 2.0 copy-done.57
  793.6 8.8 fusion.124
  802.4 12.9 multiply_bitcast_fusion.3
  815.3 4.9 fusion.142
  820.2 2.2 slice-done
  822.4 1.7 bitcast_add_fusion.3
  825.0 1.9 slice-done.2
  826.9 1.7 fusion.93
  829.6 9.8 fusion.127
  839.3 33.2 %pad_maximum_fusion = f32[1024,12288]{1,0:T(8,128)} fusion(f32[1024,4096]{1,0:T(8,128)} %fusion.143, f32[1024,4096]{1,0:T(8,128)} %fusion.124, f32[1024,1024]{1,0:T(8,128)} %fusion.142, f32[1024,3072]{1,0:T(8,128)} %fusion.127), kind=kLoop, calls=%fused_computation.1 | loop fusion | flops 37748736 | bytes 100663296 | tf_op jit(solution)/shard_map/concatenate | solution.py:234
  872.6 819.0 %reduce-scatter.3.cloned.1.call-done = f32[1024,3072]{1,0:T(8,128)} async-done(((f32[1024,12288]{1,0:T(8,128)}), f32[1024,3072]{1,0:T(8,128)}) %reduce-scatter.3.cloned.1.call-update) | async-done | bytes 12582928 | tf_op jit(solution)/shard_map/reduce_scatter | solution.py:245
  1691.7 98.3 %reduce-scatter.5.cloned.1.call-done = f32[128,3072]{1,0:T(8,128)} async-done(((f32[1024,3072]{1,0:T(8,128)}), f32[128,3072]{1,0:T(8,128)}) %reduce-scatter.5.cloned.1.call-update) | async-done | bytes 1572880 | tf_op jit(solution)/shard_map/reduce_scatter | solution.py:249
  1793.2 8.8 fusion.19
  1802.1 7.9 fusion.133
  1810.1 2.0 fusion.87
  1813.4 21.5 %all-reduce.7 = f32[13312]{0:T(1024)S(1)} all-reduce(f32[13312]{0:T(1024)S(1)} %reshape.314), channel_id=4, replica_groups=mesh['dp'=4,'shard'=8] {'dp'}, use_global_device_ids=true, to_apply=%region_21.22.clone | all-reduce | flops 13312 | bytes 106496
  1835.0 25.0 %all-reduce.8 = f32[3328]{0:T(1024)S(1)} all-reduce(f32[3328]{0:T(1024)S(1)} %dynamic-slice.2), channel_id=5, replica_groups=mesh['dp'=4,'shard'=8] {'shard'}, use_global_device_ids=true, to_apply=%region_22.23.clone | all-reduce | flops 3328 | bytes 26624
  1860.2 11.8 all-reduce.6
  1872.6 37.0 %all-gather.3.cloned.1.call-done = f32[128,12288]{1,0:T(8,128)} async-done(((f32[128,3072]{1,0:T(8,128)}), f32[128,12288]{1,0:T(8,128)}) %all-gather.3.cloned.1.call-update) | async-done | bytes 6291472 | tf_op jit(solution)/shard_map/all_gather | solution.py:253
  1909.6 5.0 multiply_reduce_fusion.1
  1915.9 4.8 add_add_fusion.2
  1920.7 14.4 psum.15
  1935.9 6.6 multiply_bitcast_fusion.1
  1942.5 3.8 copy.83
  1946.2 6.6 copy.73
  1952.9 18.9 fusion.28
  1971.8 11.6 fusion.27
  1983.4 9.7 broadcast_multiply_fusion
  1993.1 6.6 copy.78
  1999.7 9.3 fusion.135
  (188 shorter events, 25.4 us)
Async XLA Ops:
  7.2 1976.2 %copy-start = (bf16[1,96,128,128]{3,2,1,0:T(8,128)(2,1)S(1)}, bf16[1,96,128,128]{3,2,1,0:T(8,128)(2,1)}, u32[]{:S(2)}) copy-start(bf16[1,96,128,128]{3,2,1,0:T(8,128)(2,1)} %param.20) | copy-start | bytes 9437188
  7.2 1684.4 %reduce-scatter.3.cloned.1.call-start = ((), (), s32[]{:S(2)}) async-start(), calls=%async_computation.2 | async-start | bytes 62914560 | tf_op jit(solution)/shard_map/reduce_scatter | solution.py:245
  13.7 6.1 collective-permute-start
  38.2 139.0 %collective-permute-start.1 = (bf16[2,128,12288]{2,1,0:T(8,128)(2,1)}, bf16[2,128,12288]{2,1,0:T(8,128)(2,1)}, u32[]{:S(2)}, u32[]{:S(2)}) collective-permute-start(bf16[2,128,12288]{2,1,0:T(8,128)(2,1)} %get-tuple-element.31), channel_id=1, source_target_pairs={{0,2},{1,3},{2,0},{3,1},{4,6},{5,7},{6,4},{7,5},{8,10},{9,11},{10,... | collective-permute-start | bytes 18874376 | tf_op jit(solution)/shard_map/ppermute | solution.py:29
  183.3 9.2 copy-start.46
  183.3 314.0 %copy-start.37 = (f32[1664]{0:T(1024)S(1)}, f32[1664]{0:T(1024)}, u32[]{:S(2)}) copy-start(f32[1664]{0:T(1024)} %param.16) | copy-start | bytes 19972
  190.7 324.7 %collective-permute-start.2 = (bf16[4,128,12288]{2,1,0:T(8,128)(2,1)}, bf16[4,128,12288]{2,1,0:T(8,128)(2,1)}, u32[]{:S(2)}, u32[]{:S(2)}) collective-permute-start(bf16[4,128,12288]{2,1,0:T(8,128)(2,1)} %bitcast.8), channel_id=1, source_target_pairs={{0,4},{1,5},{2,6},{3,7},{4,0},{5,1},{6,2},{7,3},{8,12},{9,13},{10,... | collective-permute-start | bytes 37748744 | tf_op jit(solution)/shard_map/ppermute | solution.py:29
  507.5 50.6 %copy-start.43 = (f32[4096]{0:T(1024)}, f32[4096]{0:T(1024)S(1)}, u32[]{:S(2)}) copy-start(f32[4096]{0:T(1024)S(1)} %slice.122) | copy-start | bytes 49156
  510.6 47.5 %copy-start.35 = (f32[512]{0:T(512)}, f32[512]{0:T(512)S(1)}, u32[]{:S(2)}) copy-start(f32[512]{0:T(512)S(1)} %broadcast_multiply_fusion.1) | copy-start | bytes 6148
  512.8 45.3 %copy-start.39 = (f32[512]{0:T(512)}, f32[512]{0:T(512)S(1)}, u32[]{:S(2)}) copy-start(f32[512]{0:T(512)S(1)} %fusion.117) | copy-start | bytes 6148
  514.0 27.4 %copy-start.33 = (f32[1024]{0:T(1024)}, f32[1024]{0:T(1024)S(1)}, u32[]{:S(2)}) copy-start(f32[1024]{0:T(1024)S(1)} %get-tuple-element.49) | copy-start | bytes 12292
  514.0 27.4 %copy-start.48 = (f32[1024]{0:T(1024)}, f32[1024]{0:T(1024)S(1)}, u32[]{:S(2)}) copy-start(f32[1024]{0:T(1024)S(1)} %get-tuple-element.48) | copy-start | bytes 12292
  514.0 44.1 %copy-start.31 = (f32[1024]{0:T(1024)}, f32[1024]{0:T(1024)S(1)}, u32[]{:S(2)}) copy-start(f32[1024]{0:T(1024)S(1)} %get-tuple-element.47) | copy-start | bytes 12292
  514.0 44.1 %copy-start.50 = (f32[1024]{0:T(1024)}, f32[1024]{0:T(1024)S(1)}, u32[]{:S(2)}) copy-start(f32[1024]{0:T(1024)S(1)} %get-tuple-element.46) | copy-start | bytes 12292
  514.1 75.9 %copy-start.27 = (f32[512,8]{0,1:T(8,128)}, f32[512,8]{0,1:T(8,128)S(1)}, u32[]{:S(2)}) copy-start(f32[512,8]{0,1:T(8,128)S(1)} %get-tuple-element.54) | copy-start | bytes 49156
  514.1 75.9 %copy-start.29 = (f32[512,8]{0,1:T(8,128)}, f32[512,8]{0,1:T(8,128)S(1)}, u32[]{:S(2)}) copy-start(f32[512,8]{0,1:T(8,128)S(1)} %get-tuple-element.55) | copy-start | bytes 49156
  527.4 14.0 copy-start.2
  550.9 40.2 %collective-permute-start.3 = (bf16[512,1024]{1,0:T(8,128)(2,1)}, bf16[512,1024]{1,0:T(8,128)(2,1)}, u32[]{:S(2)}, u32[]{:S(2)}) collective-permute-start(bf16[512,1024]{1,0:T(8,128)(2,1)} %slice.167), channel_id=1, source_target_pairs={{0,1},{1,0},{2,3},{3,2},{4,5},{5,4},{6,7},{7,6},{8,9},{9,8},{10,11... | collective-permute-start | bytes 3145736 | tf_op jit(solution)/shard_map/ppermute | solution.py:41
  557.9 40.5 %collective-permute-start.4 = (bf16[512,1024]{0,1:T(8,128)(2,1)}, bf16[512,1024]{0,1:T(8,128)(2,1)}, u32[]{:S(2)}, u32[]{:S(2)}) collective-permute-start(bf16[512,1024]{0,1:T(8,128)(2,1)} %bitcast.14), channel_id=1, source_target_pairs={{0,1},{1,0},{2,3},{3,2},{4,5},{5,4},{6,7},{7,6},{8,9},{9,8},{10,11... | collective-permute-start | bytes 3145736 | tf_op jit(solution)/shard_map/ppermute | solution.py:41
  591.1 24.7 %copy-start.19 = (bf16[512,16,8]{0,2,1:T(8,128)(2,1)}, bf16[512,16,8]{0,2,1:T(8,128)(2,1)S(1)}, u32[]{:S(2)}) copy-start(bf16[512,16,8]{0,2,1:T(8,128)(2,1)S(1)} %get-tuple-element.38) | copy-start | bytes 393220
  591.1 24.7 %copy-start.21 = (bf16[512,16,8]{0,2,1:T(8,128)(2,1)}, bf16[512,16,8]{0,2,1:T(8,128)(2,1)S(1)}, u32[]{:S(2)}) copy-start(bf16[512,16,8]{0,2,1:T(8,128)(2,1)S(1)} %get-tuple-element.39) | copy-start | bytes 393220
  654.0 18.6 copy-start.52
  654.0 18.6 copy-start.53
  654.0 18.6 copy-start.55
  692.0 14.9 copy-start.18
  692.0 14.9 copy-start.23
  706.9 22.5 %copy-start.17 = (bf16[512,4096]{1,0:T(8,128)(2,1)S(1)}, bf16[512,4096]{1,0:T(8,128)(2,1)}, u32[]{:S(2)}) copy-start(bf16[512,4096]{1,0:T(8,128)(2,1)} %get-tuple-element.24) | copy-start | bytes 12582916
  706.9 22.5 %copy-start.25 = (bf16[512,1024]{1,0:T(8,128)(2,1)S(1)}, bf16[512,1024]{1,0:T(8,128)(2,1)}, u32[]{:S(2)}) copy-start(bf16[512,1024]{1,0:T(8,128)(2,1)} %copy-done.24) | copy-start | bytes 3145732
  729.4 8.2 copy-start.8
  738.8 86.2 %collective-permute-start.6 = (bf16[512,1024]{0,1:T(8,128)(2,1)}, bf16[512,1024]{0,1:T(8,128)(2,1)}, u32[]{:S(2)}, u32[]{:S(2)}) collective-permute-start(bf16[512,1024]{0,1:T(8,128)(2,1)} %bitcast.28), channel_id=1, source_target_pairs={{0,1},{1,0},{2,3},{3,2},{4,5},{5,4},{6,7},{7,6},{8,9},{9,8},{10,11... | collective-permute-start | bytes 3145736 | tf_op jit(solution)/shard_map/ppermute | solution.py:41
  739.1 27.7 %copy-start.20 = (bf16[512,16,8]{0,2,1:T(8,128)(2,1)S(1)}, bf16[512,16,8]{0,2,1:T(8,128)(2,1)}, u32[]{:S(2)}) copy-start(bf16[512,16,8]{0,2,1:T(8,128)(2,1)} %copy-done.19) | copy-start | bytes 393220
  739.1 27.7 %copy-start.22 = (bf16[512,16,8]{0,2,1:T(8,128)(2,1)S(1)}, bf16[512,16,8]{0,2,1:T(8,128)(2,1)}, u32[]{:S(2)}) copy-start(bf16[512,16,8]{0,2,1:T(8,128)(2,1)} %copy-done.21) | copy-start | bytes 393220
  766.8 11.5 copy-start.26
  766.9 11.5 copy-start.44
  777.3 42.9 %collective-permute-start.5 = (bf16[512,1024]{0,1:T(8,128)(2,1)}, bf16[512,1024]{0,1:T(8,128)(2,1)}, u32[]{:S(2)}, u32[]{:S(2)}) collective-permute-start(bf16[512,1024]{0,1:T(8,128)(2,1)} %bitcast.23), channel_id=1, source_target_pairs={{0,1},{1,0},{2,3},{3,2},{4,5},{5,4},{6,7},{7,6},{8,9},{9,8},{10,11... | collective-permute-start | bytes 3145736 | tf_op jit(solution)/shard_map/ppermute | solution.py:41
  778.3 15.2 copy-start.3
  778.3 15.2 copy-start.32
  778.3 15.2 copy-start.36
  778.3 15.2 copy-start.40
  778.4 15.2 copy-start.51
  820.2 4.2 copy-start.7
  820.2 4.2 copy-start.28
  820.2 4.2 copy-start.30
  820.2 4.6 slice-start.1
  824.2 2.7 slice-start.2
  824.4 5.2 copy-start.4
  824.4 5.2 copy-start.34
  824.4 5.2 copy-start.49
  824.8 3.8 copy-start.11
  825.0 3.7 copy-start.13
  872.6 917.4 %reduce-scatter.5.cloned.1.call-start = ((), (), s32[]{:S(2)}) async-start(), calls=%async_computation.3 | async-start | bytes 14155776 | tf_op jit(solution)/shard_map/reduce_scatter | solution.py:249
  1691.6 98.5 %copy-start.56 = (u32[32]{0:T(128)S(1)}, u32[32]{0:T(128)}, u32[]{:S(2)}) copy-start(u32[32]{0:T(128)} %constant.199) | copy-start | bytes 388
  1691.6 99.0 %copy-start.54 = (u32[32]{0:T(128)S(1)}, u32[32]{0:T(128)}, u32[]{:S(2)}) copy-start(u32[32]{0:T(128)} %constant.189) | copy-start | bytes 388
  1691.6 218.0 %all-gather.3.cloned.1.call-start = ((), (), s32[]{:S(2)}) async-start(), calls=%async_computation.4 | async-start | bytes 7864320 | tf_op jit(solution)/shard_map/all_gather | solution.py:253
  1793.2 8.9 copy-start.5
  1793.2 8.9 copy-start.12
  1793.2 8.9 copy-start.14
  1793.2 8.9 copy-start.16
  1802.1 8.0 copy-start.9
  1802.1 7.9 copy-start.42
  1810.1 3.1 copy-start.45
  1952.9 18.9 copy-start.1
  1999.7 9.3 copy-start.38
  1999.7 9.3 copy-start.47
  (7 other events, 11.1 us)
Sparse Core Ops, SparseCore 0:
  872.7 818.8 reduce-scatter.2
  1695.5 94.4 reduce-scatter.4
  1791.7 117.8 all-gather.2
